TPU v7x, 512 devices: a whole 4x8x8 slice. The times are simulated.
512 devices in a mesh: section: 2 (over core), tensor: 32 (over z, x), dp: 8 (over y).
Axes of the slice: x: 4, y: 8, z: 8, core: 2. Of those that a mesh axis runs over, the one named last changes fastest.
Arguments:
- grad_out: bfloat16 [2048, 6144], P('dp', 'tensor'), may hold values from -6 to 6
- queries: bfloat16 [2, 2048, 4096], P('section', 'dp', 'tensor'), may hold values from -40 to 40
- key_rows: bfloat16 [2, 2048, 4096], P('section', 'dp', 'tensor'), may hold values from -40 to 40
- value_rows: bfloat16 [2, 2048, 4096], P('section', 'dp', 'tensor'), may hold values from -6 to 6
- w_qkv: bfloat16 [2, 6144, 12288], P('section', 'dp', 'tensor'), may hold values from -0.078125 to 0.078125
- w_out: bfloat16 [2, 4096, 6144], P('section', 'tensor', 'dp'), may hold values from -0.09375 to 0.09375
- seg_lengths: int32 [8, 3], P('dp'), may hold values from 0 to 128, as said below
Outputs:
- input_grad: bfloat16 [2, 2048, 6144], P('section', 'dp', 'tensor')
- out_weight_grad: bfloat16 [2, 4096, 6144], P('section', 'tensor', 'dp')
Inputs may be any that keep to these rules, and one draw needn't show every extreme that they name: `seg_lengths`: each row sums to 256, holds one image of exactly 128 patches and either a second of 128 patches and an empty last slot, or two of 64 patches.
All inputs are finite; a program needn't handle non-finite values.
Results may differ from a plain program's by a relative error of at most 0.023.
Values may be sent and summed in bfloat16 or wider, within the bound.
A program may use at most 64 MiB of HBM per device.

v0:
```python
import jax
import jax.numpy as jnp
from jax import lax
from jax.sharding import PartitionSpec as P

PACK = 256
MB = 1


negative_big = -1e30


def passed_along(value, axis, steps):
    count = lax.axis_size(axis)
    first, last = (max(0, -steps), min(count, count - steps))
    return lax.ppermute(value, axis, [(source, source + steps) for source in range(first, last)])


def contract(left, right, left_dim, right_dim):
    return lax.dot_general(
        left, right, (((left_dim,), (right_dim,)), ((), ())), preferred_element_type=jnp.float32
    )


def attend_back(query_blk, key_blk, value_blk, grad_attn, same_seg, scaling):
    scores = contract(query_blk, key_blk, 1, 1) * scaling
    scores = jnp.where(same_seg, scores, negative_big)
    peak = jnp.max(scores, axis=-1, keepdims=True)
    shifted = jnp.exp(scores - peak)
    probs = shifted / jnp.sum(shifted, axis=-1, keepdims=True)
    probs_low = probs.astype(jnp.bfloat16)
    attended = jnp.dot(probs_low, value_blk, preferred_element_type=jnp.float32).astype(
        jnp.bfloat16
    )
    grad_value = contract(probs_low, grad_attn, 0, 0).astype(jnp.bfloat16)
    grad_probs = contract(grad_attn, value_blk, 1, 1)
    centred = jnp.sum(probs * grad_probs, axis=-1, keepdims=True)
    grad_scores = (probs * (grad_probs - centred) * scaling).astype(jnp.bfloat16)
    grad_query = jnp.dot(grad_scores, key_blk, preferred_element_type=jnp.float32).astype(
        jnp.bfloat16
    )
    grad_key = contract(grad_scores, query_blk, 0, 0).astype(jnp.bfloat16)
    return (attended, grad_query, grad_key, grad_value)


def per_device(grad_out, queries, key_rows, value_rows, w_qkv, w_out, seg_lengths):
    sections = lax.axis_size("section")
    section_index = lax.axis_index("section")
    head_index = lax.axis_index("tensor")
    width = grad_out.shape[1]
    qkv_full, out_full = (
        lax.all_gather(w_qkv, "dp", axis=1, tiled=True),
        lax.all_gather(w_out, "dp", axis=2, tiled=True),
    )
    proj_in = qkv_full[0]
    proj_out = out_full[0]
    head_dim = proj_out.shape[0]
    full_width = proj_out.shape[1]
    scaling = head_dim ** (-0.5)
    seg_ends = jnp.cumsum(seg_lengths, axis=1)
    position = jnp.arange(PACK, dtype=jnp.int32)
    seg_table = jnp.sum((position[None, :, None] >= seg_ends[:, None, :]).astype(jnp.int32), axis=2)
    offset = sections - 1 - section_index
    carried = jnp.zeros((PACK, width), jnp.bfloat16)
    result = jnp.zeros((MB * PACK, width), jnp.bfloat16)
    grad_acc = jnp.zeros((head_dim, full_width), jnp.float32)
    for step_index in range(MB + sections - 1):
        micro = step_index - offset
        active = (micro >= 0) & (micro < MB)
        which = jnp.clip(micro, 0, MB - 1)
        incoming = jnp.where(section_index == sections - 1, grad_out, carried)
        whole = lax.all_gather(incoming, "tensor", axis=1, tiled=True)
        query_blk = queries[0]
        key_blk = key_rows[0]
        value_blk = value_rows[0]
        seg_ids = lax.dynamic_index_in_dim(seg_table, which, 0, keepdims=False)
        same_seg = seg_ids[:, None] == seg_ids[None, :]
        grad_attn = contract(whole, proj_out, 1, 1).astype(jnp.bfloat16)
        attended, grad_query, grad_key, grad_value = attend_back(
            query_blk, key_blk, value_blk, grad_attn, same_seg, scaling
        )
        combined = jnp.concatenate([grad_query, grad_key, grad_value], axis=1)
        head_term = contract(combined, proj_in, 1, 1)
        summed = lax.psum(head_term.astype(jnp.bfloat16), "tensor").astype(jnp.float32)
        share = lax.dynamic_slice_in_dim(summed, head_index * width, width, 1)
        block_grad = (incoming.astype(jnp.float32) + share).astype(jnp.bfloat16)
        result = jnp.where(active, block_grad, result)
        grad_acc = grad_acc + jnp.where(active, contract(attended, whole, 0, 0), 0.0)
        carried = passed_along(block_grad, "section", -1)
    weight_share = lax.psum_scatter(
        grad_acc.astype(jnp.bfloat16), "dp", scatter_dimension=1, tiled=True
    )
    return (result[None], weight_share[None])


def solution(mesh):
    return jax.shard_map(
        per_device,
        mesh=mesh,
        in_specs=(
            P("dp", "tensor"),
            P("section", "dp", "tensor"),
            P("section", "dp", "tensor"),
            P("section", "dp", "tensor"),
            P("section", "dp", "tensor"),
            P("section", "tensor", "dp"),
            P("dp", None),
        ),
        out_specs=(P("section", "dp", "tensor"), P("section", "tensor", "dp")),
        check_vma=False,
    )
```

profile of v0, /device:TPU:6, one launch (start us, length us, event | category | flops | bytes accessed | tf_op | source)
XLA Modules:
  0.0 695.8 jit_solution(12003352529557310799)
XLA Ops:
  7.2 0.7 all-gather.7.cloned.1.call-update
  8.0 0.7 broadcast_select_fusion.1
  8.7 0.7 all-gather.9.cloned.1.call-update
  9.4 0.8 reduce_window_sum.11
  10.4 1.1 fusion.49
  11.5 45.2 %all-gather.7.cloned.1.call-done = bf16[1,128,6144]{2,1,0:T(8,128)(2,1)} async-done(((bf16[1,128,768]{2,1,0:T(8,128)(2,1)}), bf16[1,128,6144]{2,1,0:T(8,128)(2,1)}) %all-gather.7.cloned.1.call-update) | async-done | bytes 1572880 | tf_op jit(solution)/shard_map/all_gather | solution.py:53
  56.7 86.7 %all-gather.5.cloned.1.call-done = bf16[256,6144]{0,1:T(8,128)(2,1)} async-done(((bf16[256,192]{0,1:T(8,128)(2,1)}), bf16[256,6144]{0,1:T(8,128)(2,1)}) %all-gather.5.cloned.1.call-update) | async-done | bytes 3145744 | tf_op jit(solution)/shard_map/all_gather | solution.py:72
  143.4 3.4 fusion.9
  146.8 0.2 multiply_reduce_fusion.1
  147.3 0.2 convolution_convert_fusion.8
  147.6 0.2 convolution_convert_fusion.6
  147.7 57.7 %all-gather.9.cloned.1.call-done = bf16[1,6144,384]{2,1,0:T(8,128)(2,1)} async-done(((bf16[1,768,384]{2,1,0:T(8,128)(2,1)}), bf16[1,6144,384]{2,1,0:T(8,128)(2,1)}) %all-gather.9.cloned.1.call-update) | async-done | bytes 4718608 | tf_op jit(solution)/shard_map/all_gather | solution.py:52
  205.5 5.9 convolution_convert_fusion.1
  211.5 168.1 %all-reduce.3.cloned.1.call-done = bf16[256,6144]{0,1:T(8,128)(2,1)} async-done(((bf16[256,6144]{0,1:T(8,128)(2,1)}), bf16[256,6144]{0,1:T(8,128)(2,1)}) %all-reduce.3.cloned.1.call-update) | async-done | bytes 3145744 | tf_op jit(solution)/shard_map/psum | solution.py:84
  379.6 0.9 add_convert_fusion.1
  380.5 1.3 collective-permute-start
  381.8 1.9 collective-permute-done
  383.7 0.7 broadcast_select_fusion
  384.4 82.7 %all-gather.11.cloned.1.call-done = bf16[256,6144]{0,1:T(8,128)(2,1)} async-done(((bf16[256,192]{0,1:T(8,128)(2,1)}), bf16[256,6144]{0,1:T(8,128)(2,1)}) %all-gather.11.cloned.1.call-update) | async-done | bytes 3145744 | tf_op jit(solution)/shard_map/all_gather | solution.py:72
  467.2 2.9 fusion.12
  470.1 0.2 convolution_convert_fusion.3
  470.3 0.2 multiply_reduce_fusion
  470.8 0.2 convolution_convert_fusion.5
  471.0 5.9 convolution_convert_fusion
  477.0 0.2 convolution_convert_fusion.2
  477.3 1.6 copy-done.1
  478.8 1.2 convolution_select_fusion.1
  480.0 0.7 copy-done.2
  480.7 2.3 fusion.1
  483.1 160.8 %all-reduce.5.cloned.1.call-done = bf16[256,6144]{0,1:T(8,128)(2,1)} async-done(((bf16[256,6144]{0,1:T(8,128)(2,1)}), bf16[256,6144]{0,1:T(8,128)(2,1)}) %all-reduce.5.cloned.1.call-update) | async-done | bytes 3145744 | tf_op jit(solution)/shard_map/psum | solution.py:84
  644.0 1.6 fusion.28
  645.5 43.4 %reduce-scatter.2.cloned.1.call-done = bf16[128,768]{1,0:T(8,128)(2,1)} async-done(((bf16[128,6144]{1,0:T(8,128)(2,1)}), bf16[128,768]{1,0:T(8,128)(2,1)}) %reduce-scatter.2.cloned.1.call-update) | async-done | bytes 196624 | tf_op jit(solution)/shard_map/reduce_scatter | solution.py:90
  (36 shorter events, 1.1 us)
Async XLA Ops:
  7.2 139.7 %copy-start = (bf16[1,256,128]{2,1,0:T(8,128)(2,1)S(1)}, bf16[1,256,128]{2,1,0:T(8,128)(2,1)}, u32[]{:S(2)}) copy-start(bf16[1,256,128]{2,1,0:T(8,128)(2,1)} %param.10) | copy-start | bytes 196612
  7.2 49.5 %all-gather.7.cloned.1.call-start = ((), (), s32[]{:S(2)}) async-start(), calls=%async_computation.2 | async-start | bytes 1769472 | tf_op jit(solution)/shard_map/all_gather | solution.py:53
  7.9 135.5 %all-gather.5.cloned.1.call-start = ((), (), s32[]{:S(2)}) async-start(), calls=%async_computation.1 | async-start | bytes 3244032 | tf_op jit(solution)/shard_map/all_gather | solution.py:72
  8.7 196.8 %all-gather.9.cloned.1.call-start = ((), (), s32[]{:S(2)}) async-start(), calls=%async_computation.3 | async-start | bytes 5308416 | tf_op jit(solution)/shard_map/all_gather | solution.py:52
  9.4 370.2 %all-reduce.3.cloned.1.call-start = ((), (), s32[]{:S(2)}) async-start(), calls=%async_computation.4 | async-start | bytes 6291456 | tf_op jit(solution)/shard_map/psum | solution.py:84
  11.5 135.6 %copy-start.8 = (bf16[1,256,128]{2,1,0:T(8,128)(2,1)S(1)}, bf16[1,256,128]{2,1,0:T(8,128)(2,1)}, u32[]{:S(2)}) copy-start(bf16[1,256,128]{2,1,0:T(8,128)(2,1)} %param.8) | copy-start | bytes 196612
  11.5 135.8 %copy-start.9 = (bf16[1,256,128]{2,1,0:T(8,128)(2,1)S(1)}, bf16[1,256,128]{2,1,0:T(8,128)(2,1)}, u32[]{:S(2)}) copy-start(bf16[1,256,128]{2,1,0:T(8,128)(2,1)} %param.9) | copy-start | bytes 196612
  211.4 168.2 %copy-start.4 = (bf16[256,192]{0,1:T(8,128)(2,1)S(1)}, bf16[256,192]{0,1:T(8,128)(2,1)}, u32[]{:S(2)}) copy-start(bf16[256,192]{0,1:T(8,128)(2,1)} %param.7) | copy-start | bytes 294916
  211.4 255.8 %copy-start.3 = (bf16[1,128,6144]{2,1,0:T(8,128)(2,1)S(1)}, bf16[1,128,6144]{2,1,0:T(8,128)(2,1)}, u32[]{:S(2)}) copy-start(bf16[1,128,6144]{2,1,0:T(8,128)(2,1)} %all-gather.7.cloned.1.call-done) | copy-start | bytes 4718596
  211.4 255.8 %all-gather.11.cloned.1.call-start = ((), (), s32[]{:S(2)}) async-start(), calls=%async_computation.5 | async-start | bytes 3244032 | tf_op jit(solution)/shard_map/all_gather | solution.py:72
  380.5 90.0 %copy-start.6 = (bf16[256,192]{0,1:T(8,128)(2,1)}, bf16[256,192]{0,1:T(8,128)(2,1)S(1)}, u32[]{:S(2)}) copy-start(bf16[256,192]{0,1:T(8,128)(2,1)S(1)} %add_convert_fusion.1) | copy-start | bytes 294916
  380.5 3.2 collective-permute-start
  384.4 259.6 %all-reduce.5.cloned.1.call-start = ((), (), s32[]{:S(2)}) async-start(), calls=%async_computation.6 | async-start | bytes 6291456 | tf_op jit(solution)/shard_map/psum | solution.py:84
  477.0 1.9 copy-start.1
  477.0 212.0 %reduce-scatter.2.cloned.1.call-start = ((), (), s32[]{:S(2)}) async-start(), calls=%async_computation.7 | async-start | bytes 1769472 | tf_op jit(solution)/shard_map/reduce_scatter | solution.py:90
  478.8 1.9 copy-start.2
  480.7 163.2 %copy-start.5 = (bf16[256,192]{0,1:T(8,128)(2,1)S(1)}, bf16[256,192]{0,1:T(8,128)(2,1)}, u32[]{:S(2)}) copy-start(bf16[256,192]{0,1:T(8,128)(2,1)} %broadcast_select_fusion) | copy-start | bytes 294916
  480.7 163.2 %copy-start.7 = (bf16[256,192]{0,1:T(8,128)(2,1)S(1)}, bf16[256,192]{0,1:T(8,128)(2,1)}, u32[]{:S(2)}) copy-start(bf16[256,192]{0,1:T(8,128)(2,1)} %copy-done.6) | copy-start | bytes 294916
Sparse Core Ops, SparseCore 0:
  10.1 46.5 all-gather.6
  60.4 82.9 all-gather.4
  145.5 59.8 all-gather.8
  211.5 167.9 all-reduce.2
  384.5 82.6 all-gather.10
  477.1 166.8 all-reduce.4
  647.4 41.5 reduce-scatter.1
where the time goes:
time: 696 us
  waiting for transfers between devices  648 us (93%)
  matrix products  24.6 us (4%)
  between operations  14.3 us (2%)
    psum x2, waiting for transfers between devices, per_device(): lax.psum(head_term.astype(jnp.bfloat16), 'tensor').astype(jnp.float32)  329 us
    all_gather x2, waiting for transfers between devices, per_device(): whole = lax.all_gather(incoming, 'tensor', axis=1, tiled=True)  169 us
    all_gather x1, waiting for transfers between devices, per_device(): lax.all_gather(w_qkv, 'dp', axis=1, tiled=True)  57.7 us
    all_gather x1, waiting for transfers between devices, per_device(): lax.all_gather(w_out, 'dp', axis=2, tiled=True)  45.2 us
    reduce_scatter x1, waiting for transfers between devices, per_device(): lax.psum_scatter(grad_acc.astype(jnp.bfloat16), 'dp', scatter_dimension=1...  43.4 us
    dot_general x13, matrix products, contract(): lax.dot_general(left, right, (((left_dim,), (right_dim,)), ((), ())), pre...  23.9 us
  transfers between devices with their start and end apart: 8, of which 8 were waited for; matrix products, arithmetic and copies ran while one was open for 2% of the time, Pallas kernels for 0%

commit v1 on v0

v1 whole, which is shorter than its diff:
```python
import jax
import jax.numpy as jnp
from jax import lax
from jax.experimental import pallas as pl
from jax.experimental.pallas import tpu as pltpu
from jax.sharding import PartitionSpec as P

MESH = pl.DeviceIdType.MESH
NX, NZ, NY = 4, 8, 8
TOK, HD, COLS = 256, 128, 192
WIDE = NX * COLS
RING = (1, 7, 2, 6, 3, 5, 4)
negative_big = -1e30
F32, BF16 = jnp.float32, jnp.bfloat16


def dot_nt(left, right):
    return lax.dot_general(left, right, (((1,), (1,)), ((), ())), preferred_element_type=F32)


def dot_nn(left, right):
    return lax.dot_general(left, right, (((1,), (0,)), ((), ())), preferred_element_type=F32)


def kernel(seg_ref, up_in, q_ref, k_ref, v_ref, wq_ref, wo_ref, og_ref, ow_ref,
           up, wo, wq, ht, rs1, snd2, rs2, zs, rz, gs, gr, comb, att, hop, fin,
           agz_s, agz_r, agx_s, agx_r, wo_s, wo_r, wq_s, wq_r, rs1_s, rs1_r, rs2_s, rs2_r,
           rz_s, rz_r, g_s, g_r, hop_s, hop_r, gate):
    s = lax.axis_index("section")
    t = lax.axis_index("tensor")
    y = lax.axis_index("dp")
    z, x = t // NX, t % NX
    flip, mirror, across = x + 1 - 2 * (x % 2), NX - 1 - x, (x + 2) % NX

    def pair(k):
        return (flip, mirror) if k % 2 == 0 else (mirror, flip)

    def row(value):
        return {"tensor": z * NX + value}

    def column(value):
        return {"tensor": value * NX + x}

    def ring(value):
        return {"dp": value}

    def copy(src, dst, ss, rs, dev):
        return pltpu.make_async_remote_copy(src_ref=src, dst_ref=dst, send_sem=ss, recv_sem=rs,
                                            device_id=dev, device_id_type=MESH)

    def arrived(dst, rs):
        copy(dst, dst, hop_s.at[0], rs, {"section": 1 - s}).wait_recv()

    barrier = pltpu.get_barrier_semaphore()
    peers = [row(flip), row(mirror), {"section": 1 - s}]
    peers += [column((z + k) % NZ) for k in range(1, NZ)]
    peers += [ring((y + k) % NY) for k in range(1, NY)]
    for peer in peers:
        pl.semaphore_signal(barrier, inc=1, device_id=peer, device_id_type=MESH)
    pl.semaphore_wait(barrier, len(peers))

    def ag_z(src, k):
        return copy(src, up.at[z, x], agz_s.at[k], agz_r.at[k], column((z + k) % NZ))

    def ag_x(src, k):
        zk = (z + NZ - k) % NZ
        own = src if k == 0 else up.at[zk, x]
        near, far = pair(k)
        return (copy(own, up.at[zk, x], agx_s.at[0, k], agx_r.at[0, k], row(near)),
                copy(own, up.at[zk, x], agx_s.at[1, k], agx_r.at[1, k], row(far)),
                copy(up.at[zk, near], up.at[zk, near], agx_s.at[2, k], agx_r.at[2, k], row(far)))

    def take_z(src, k):
        if k:
            arrived(up.at[(z + NZ - k) % NZ, x], agz_r.at[k])
        for each in ag_x(src, k)[:2]:
            each.start()

    def relay_x(src, k):
        arrived(up.at[(z + NZ - k) % NZ, pair(k)[0]], agx_r.at[0, k])
        ag_x(src, k)[2].start()

    def finish_x(k):
        zk = (z + NZ - k) % NZ
        arrived(up.at[zk, pair(k)[1]], agx_r.at[1, k])
        arrived(up.at[zk, across], agx_r.at[2, k])

    def hops(own, full, half, ss, rs, way, step):
        toward = (y + 1) % NY if way == 0 else (y + NY - 1) % NY
        block = (y + NY - step) % NY if way == 0 else (y + step) % NY
        src, dst = (own if step == 0 else full.at[block]), full.at[block]
        if step == 3:
            part = pl.ds(half * way, half)
            src, dst = full.at[block, part], full.at[block, part]
        return copy(src, dst, ss.at[way, step], rs.at[way, step], ring(toward))

    def ring_wait(full, half, rs, way, step):
        block = (y + NY - step - 1) % NY if way == 0 else (y + step + 1) % NY
        ref = full.at[block, pl.ds(half * way, half)] if step == 3 else full.at[block]
        arrived(ref, rs.at[way, step])

    def wo_hop(step, way):
        return hops(wo_ref.at[0], wo, HD // 2, wo_s, wo_r, way, step)

    def wq_hop(step, way):
        return hops(wq_ref.at[0], wq, WIDE // 2, wq_s, wq_r, way, step)

    def wo_step(step):
        for way in (0, 1):
            if step:
                ring_wait(wo, HD // 2, wo_r, way, step - 1)
            if step < 4:
                wo_hop(step, way).start()

    def wq_step(step):
        for way in (0, 1):
            if step:
                ring_wait(wq, WIDE // 2, wq_r, way, step - 1)
            if step < 4:
                wq_hop(step, way).start()

    def early(src):
        for k in RING:
            ag_z(src, k).start()
        wo_step(0)
        take_z(src, 0)
        take_z(src, 1)
        take_z(src, 7)
        relay_x(src, 0)
        wo_step(1)
        take_z(src, 2)
        take_z(src, 6)
        relay_x(src, 1)
        relay_x(src, 7)
        wo_step(2)
        take_z(src, 3)
        take_z(src, 5)
        relay_x(src, 2)
        relay_x(src, 6)
        wo_step(3)
        wq_step(0)
        take_z(src, 4)
        for k in (3, 5, 4):
            relay_x(src, k)
        wo_step(4)
        for k in range(NZ):
            finish_x(k)
        up[z, x] = src[...]
        wq_step(1)

    def late(src):
        pl.semaphore_wait(gate, 1)
        for step in range(5):
            wo_step(step)
            wq_step(step)
        arrived(hop, hop_r.at[0])
        for k in RING:
            ag_z(src, k).start()
        order = (0,) + RING
        for place, k in enumerate(order):
            take_z(src, k)
            if place:
                relay_x(src, order[place - 1])
        relay_x(src, order[-1])
        for k in range(NZ):
            finish_x(k)
        up[z, x] = src[...]

    wo[y] = wo_ref[0]
    wq[y] = wq_ref[0]

    @pl.when(s == 1)
    def _():
        early(up_in)

    @pl.when(s == 0)
    def _():
        late(hop)

    scaling = HD ** -0.5
    grad_t = jnp.zeros((HD, TOK), F32)
    for j in range(NZ):
        grad_t = grad_t + dot_nn(wo[j], up[j].reshape(WIDE, TOK))
    grad_attn = grad_t.T.astype(BF16)
    end0 = seg_ref[0, 0]
    end1 = end0 + seg_ref[0, 1]
    end2 = end1 + seg_ref[0, 2]

    def seg_of(axis):
        place = lax.broadcasted_iota(jnp.int32, (TOK, TOK), axis)
        return (jnp.where(place >= end0, 1, 0) + jnp.where(place >= end1, 1, 0)
                + jnp.where(place >= end2, 1, 0))

    q, k, v = q_ref[0], k_ref[0], v_ref[0]
    scores = jnp.where(seg_of(0) == seg_of(1), dot_nt(q, k) * scaling, negative_big)
    shifted = jnp.exp(scores - jnp.max(scores, axis=1, keepdims=True))
    probs = shifted / jnp.sum(shifted, axis=1, keepdims=True)
    att[...] = dot_nn(probs.astype(BF16), v).T.astype(BF16)
    comb[:, 2 * HD:] = dot_nn(probs.T.astype(BF16), grad_attn).astype(BF16)
    grad_probs = dot_nt(grad_attn, v)
    centred = jnp.sum(probs * grad_probs, axis=1, keepdims=True)
    grad_scores = probs * (grad_probs - centred) * scaling
    comb[:, :HD] = dot_nn(grad_scores.astype(BF16), k).astype(BF16)
    comb[:, HD:2 * HD] = dot_nn(grad_scores.T.astype(BF16), q).astype(BF16)

    def grad_copy(m):
        return copy(gs.at[m], gr.at[m], g_s.at[m], g_r.at[m], ring((y + m) % NY))

    def weight_grad():
        def one(m, _):
            j = (y + m) % NY
            gs[m] = dot_nt(att[...], up[j].reshape(WIDE, TOK)).astype(BF16)

            @pl.when(m > 0)
            def _():
                grad_copy(m).start()
            return 0

        lax.fori_loop(0, NY, one, 0)

    def x_copies(m):
        j = (y + m) % NY
        near, far = pair(m)
        return (copy(ht.at[j, across], rs1.at[m, 1], rs1_s.at[1, m], rs1_r.at[1, m], row(near)),
                copy(ht.at[j, near], rs1.at[m, 0], rs1_s.at[0, m], rs1_r.at[0, m], row(near)),
                copy(snd2.at[m], rs2.at[m], rs2_s.at[m], rs2_r.at[m], row(far)))

    def z_copy(m):
        return copy(zs.at[m], rz.at[z], rz_s.at[m], rz_r.at[z], column((y + m) % NY))

    def term(m):
        j = (y + m) % NY

        def one(i, _):
            ht[j, i] = dot_nt(wq[j, pl.ds(pl.multiple_of(i * COLS, COLS), COLS)], comb[...]).astype(BF16)
            return 0

        lax.fori_loop(0, NX, one, 0)
        for each in x_copies(m)[:2]:
            each.start()

    def second(m):
        j = (y + m) % NY
        arrived(rs1.at[m, 1], rs1_r.at[1, m])
        snd2[m] = (ht[j, pair(m)[1]].astype(F32) + rs1[m, 1].astype(F32)).astype(BF16)
        x_copies(m)[2].start()

    def third(m):
        j = (y + m) % NY
        arrived(rs1.at[m, 0], rs1_r.at[0, m])
        arrived(rs2.at[m], rs2_r.at[m])
        total = ht[j, x].astype(F32) + rs1[m, 0].astype(F32) + rs2[m].astype(F32)
        zs[m] = total.astype(BF16)

        @pl.when(j != z)
        def _():
            z_copy(m).start()

        @pl.when(j == z)
        def _():
            fin[...] = total

    def at_section(which, step, *args):
        @pl.when(s == which)
        def _():
            step(*args)

    at_section(1, wq_step, 2)
    at_section(0, weight_grad)
    order = (0,) + RING
    for place, m in enumerate(order):
        if place == 3:
            at_section(1, wq_step, 3)
        if place == 5:
            at_section(1, wq_step, 4)
        term(m)
        if place >= 1:
            second(order[place - 1])
        if place >= 2:
            third(order[place - 2])

    @pl.when(s == 1)
    def _():
        pl.semaphore_signal(gate, inc=1, device_id={"section": 0}, device_id_type=MESH)

    second(order[-1])
    third(order[-2])
    third(order[-1])
    total = fin[...] + up[z, x].astype(F32)
    for k in RING:
        src = (z + k) % NZ
        arrived(rz.at[src], rz_r.at[src])
        total = total + rz[src].astype(F32)
    og_ref[...] = total.astype(BF16)

    @pl.when(s == 1)
    def _():
        copy(og_ref, hop, hop_s.at[0], hop_r.at[0], {"section": 0}).start()
        weight_grad()

    summed = gs[0].astype(F32)
    for m in range(1, NY):
        arrived(gr.at[m], g_r.at[m])
        summed = summed + gr[m].astype(F32)
    ow_ref[...] = summed.astype(BF16)

    for k in RING:
        ag_z(up_in, k).wait_send()
        grad_copy(k).wait_send()
    for k in range(NZ):
        for each in ag_x(up_in, k) + x_copies(k):
            each.wait_send()

        @pl.when((y + k) % NY != z)
        def _():
            z_copy(k).wait_send()
    for step in range(4):
        for way in (0, 1):
            wo_hop(step, way).wait_send()
            wq_hop(step, way).wait_send()

    @pl.when(s == 1)
    def _():
        copy(og_ref, hop, hop_s.at[0], hop_r.at[0], {"section": 0}).wait_send()


def per_device(grad_out, queries, key_rows, value_rows, w_qkv, w_out, seg_lengths):
    vmem = pl.BlockSpec(memory_space=pltpu.VMEM)
    dma = pltpu.SemaphoreType.DMA
    piece = (COLS, TOK)
    grad, weight = pl.pallas_call(
        kernel,
        out_shape=(jax.ShapeDtypeStruct(piece, BF16), jax.ShapeDtypeStruct((HD, WIDE), BF16)),
        in_specs=[pl.BlockSpec(memory_space=pltpu.SMEM)] + [vmem] * 6,
        out_specs=(vmem, vmem),
        scratch_shapes=[
            pltpu.VMEM((NZ, NX) + piece, BF16),
            pltpu.VMEM((NY, HD, WIDE), BF16),
            pltpu.VMEM((NY, WIDE, 3 * HD), BF16),
            pltpu.VMEM((NZ, NX) + piece, BF16),
            pltpu.VMEM((NZ, 2) + piece, BF16),
            pltpu.VMEM((NZ,) + piece, BF16),
            pltpu.VMEM((NZ,) + piece, BF16),
            pltpu.VMEM((NZ,) + piece, BF16),
            pltpu.VMEM((NZ,) + piece, BF16),
            pltpu.VMEM((NY, HD, WIDE), BF16),
            pltpu.VMEM((NY, HD, WIDE), BF16),
            pltpu.VMEM((TOK, 3 * HD), BF16),
            pltpu.VMEM((HD, TOK), BF16),
            pltpu.VMEM(piece, BF16),
            pltpu.VMEM(piece, F32),
            dma((NZ,)), dma((NZ,)), dma((3, NZ)), dma((3, NZ)),
            dma((2, 4)), dma((2, 4)), dma((2, 4)), dma((2, 4)),
            dma((2, NZ)), dma((2, NZ)), dma((NZ,)), dma((NZ,)),
            dma((NZ,)), dma((NZ,)), dma((NY,)), dma((NY,)), dma((1,)), dma((1,)),
            pltpu.SemaphoreType.REGULAR,
        ],
        compiler_params=pltpu.CompilerParams(collective_id=0, has_side_effects=True),
    )(seg_lengths, grad_out.T, queries, key_rows, value_rows, w_qkv, w_out)
    return grad.T[None], weight[None]


def solution(mesh):
    return jax.shard_map(
        per_device,
        mesh=mesh,
        in_specs=(
            P("dp", "tensor"),
            P("section", "dp", "tensor"),
            P("section", "dp", "tensor"),
            P("section", "dp", "tensor"),
            P("section", "dp", "tensor"),
            P("section", "tensor", "dp"),
            P("dp", None),
        ),
        out_specs=(P("section", "dp", "tensor"), P("section", "tensor", "dp")),
        check_vma=False,
    )
```

time: 696 us -> 190 us (0.27)
  the two profiles are of different devices: /device:TPU:6 before, /device:TPU:32 now
where the time goes in v1:
time: 190 us
  Pallas kernels  187 us (98%)
  local copies, waits for them, and re-layouts  2.26 us (1%)
    pallas_call x1, Pallas kernels, per_device(): pl.pallas_call(kernel, out_shape=(jax.ShapeDtypeStruct(piece, BF16), jax....  187 us

profile of v1, /device:TPU:32, one launch (start us, length us, event | category | flops | bytes accessed | tf_op | source)
XLA Modules:
  0.0 190.1 jit_solution(12150759603095547205)
XLA Ops:
  0.6 187.2 %shard_map.86 = (bf16[192,256]{1,0:T(8,128)(2,1)}, bf16[128,768]{1,0:T(8,128)(2,1)}) custom-call(s32[1,3]{1,0:T(1,128)} %seg_ref.1, bf16[192,256]{1,0:T(8,128)(2,1)} %bitcast.7, bf16[1,256,128]{2,1,0:T(8,128)(2,1)} %q_ref.1, bf16[1,256,128]{2,1,0:T(8,128)(2,1)} %k_ref.1, bf16[1,256,128]{2,1,0:T(8,128)(2,1)} %v_ref.1, bf16[1,768,384]{2,1,0:T(8,128)(2,1)} %wq_ref.1, ...), custom_call_target="tpu_custom_call" | custom-call | tf_op jit(solution)/shard_map/pallas_call | solution.py:331
  187.8 0.0 copy-start
  187.8 1.6 copy.11
  189.4 0.0 copy-done
  189.4 0.7 copy.12
Async XLA Ops:
  187.8 1.6 copy-start

commit v2 on v1

v2 whole, which is shorter than its diff:
```python
import jax
import jax.numpy as jnp
from jax import lax
from jax.experimental import pallas as pl
from jax.experimental.pallas import tpu as pltpu
from jax.sharding import PartitionSpec as P

MESH = pl.DeviceIdType.MESH
NX, NZ, NY = 4, 8, 8
TOK, HD, COLS = 256, 128, 192
WIDE = NX * COLS
RING = (1, 7, 2, 6, 3, 5, 4)
FAR = (4, 3, 5, 2, 6, 1, 7)
LAGS = (3, 6)
CHUNK = 256
negative_big = -1e30
F32, BF16 = jnp.float32, jnp.bfloat16


def dot_nt(left, right):
    return lax.dot_general(left, right, (((1,), (1,)), ((), ())), preferred_element_type=F32)


def dot_nn(left, right):
    return lax.dot_general(left, right, (((1,), (0,)), ((), ())), preferred_element_type=F32)


def kernel(seg_ref, up_in, q_ref, k_ref, v_ref, wq_ref, wo_ref, og_ref, ow_ref,
           up, wo, wq, ht, rs1, snd2, rs2, zs, rz, gs, gr, comb, att, low, prob, hop, fin,
           agz_s, agz_r, agx_s, agx_r, wo_s, wo_r, wq_s, wq_r, rs1_s, rs1_r, rs2_s, rs2_r,
           rz_s, rz_r, g_s, g_r, hop_s, hop_r, gate):
    s = lax.axis_index("section")
    t = lax.axis_index("tensor")
    y = lax.axis_index("dp")
    z, x = t // NX, t % NX
    flip, mirror, across = x + 1 - 2 * (x % 2), NX - 1 - x, (x + 2) % NX

    def pair(k):
        return (flip, mirror) if k % 2 == 0 else (mirror, flip)

    def row(value):
        return {"tensor": z * NX + value}

    def column(value):
        return {"tensor": value * NX + x}

    def ring(value):
        return {"dp": value}

    def copy(src, dst, ss, rs, dev):
        return pltpu.make_async_remote_copy(src_ref=src, dst_ref=dst, send_sem=ss, recv_sem=rs,
                                            device_id=dev, device_id_type=MESH)

    def arrived(dst, rs):
        copy(dst, dst, hop_s.at[0], rs, {"section": 1 - s}).wait_recv()

    barrier = pltpu.get_barrier_semaphore()
    peers = [row(flip), row(mirror), {"section": 1 - s}]
    peers += [column((z + k) % NZ) for k in range(1, NZ)]
    peers += [ring((y + k) % NY) for k in range(1, NY)]
    for peer in peers:
        pl.semaphore_signal(barrier, inc=1, device_id=peer, device_id_type=MESH)
    pl.semaphore_wait(barrier, len(peers))

    def ag_z(src, k):
        return copy(src, up.at[z, x], agz_s.at[k], agz_r.at[k], column((z + k) % NZ))

    def ag_x(src, k):
        zk = (z + NZ - k) % NZ
        own = src if k == 0 else up.at[zk, x]
        near, far = pair(k)
        return (copy(own, up.at[zk, x], agx_s.at[0, k], agx_r.at[0, k], row(near)),
                copy(own, up.at[zk, x], agx_s.at[1, k], agx_r.at[1, k], row(far)),
                copy(up.at[zk, near], up.at[zk, near], agx_s.at[2, k], agx_r.at[2, k], row(far)))

    def take_z(src, k):
        if k:
            arrived(up.at[(z + NZ - k) % NZ, x], agz_r.at[k])
        for each in ag_x(src, k)[:2]:
            each.start()

    def relay_x(src, k):
        arrived(up.at[(z + NZ - k) % NZ, pair(k)[0]], agx_r.at[0, k])
        ag_x(src, k)[2].start()

    def finish_x(k):
        zk = (z + NZ - k) % NZ
        arrived(up.at[zk, pair(k)[1]], agx_r.at[1, k])
        arrived(up.at[zk, across], agx_r.at[2, k])

    streams = [(wo_ref, wo, 0, HD, wo_s, wo_r)]
    for part in range(WIDE // CHUNK):
        streams.append((wq_ref, wq, part * CHUNK, CHUNK, wq_s.at[part], wq_r.at[part]))

    def rows_of(stream, step, way):
        low_row, size = stream[2], stream[3]
        if step == 3:
            low_row, size = low_row + size // 2 * way, size // 2
        return pl.ds(low_row, size)

    def ring_hop(stream, step, way):
        own, full, _, _, ss, rs = stream
        toward = (y + 1) % NY if way == 0 else (y + NY - 1) % NY
        block = (y + NY - step) % NY if way == 0 else (y + step) % NY
        part = rows_of(stream, step, way)
        dst = full.at[block, part]
        src = own.at[0, part] if step == 0 else dst
        return copy(src, dst, ss.at[way, step], rs.at[way, step], ring(toward))

    def ring_step(index, step):
        stream = streams[index]
        for way in (0, 1):
            if step:
                block = (y + NY - step) % NY if way == 0 else (y + step) % NY
                arrived(stream[1].at[block, rows_of(stream, step - 1, way)], stream[5].at[way, step - 1])
            if step < 4:
                ring_hop(stream, step, way).start()

    def parts_step(step):
        for index in (1, 2, 3):
            ring_step(index, step)

    def early(src):
        for k in FAR:
            ag_z(src, k).start()
        ring_step(0, 0)
        ring_step(1, 0)
        take_z(src, 0)
        softmax()
        ring_step(0, 1)
        ring_step(2, 0)
        relay_x(src, 0)
        for place, k in enumerate(FAR):
            take_z(src, k)
            if place >= 1:
                relay_x(src, FAR[place - 1])
            if place == 1:
                ring_step(0, 2)
                ring_step(3, 0)
            if place == 3:
                ring_step(0, 3)
                ring_step(1, 1)
            if place == 5:
                ring_step(2, 1)
        relay_x(src, FAR[-1])
        ring_step(3, 1)
        ring_step(0, 4)
        up[z, x] = src[...]

    def late(src):
        softmax()
        pl.semaphore_wait(gate, 1)
        for step in range(5):
            ring_step(0, step)
            parts_step(step)
        arrived(hop, hop_r.at[0])
        for k in FAR:
            ag_z(src, k).start()
        take_z(src, 0)
        relay_x(src, 0)
        for place, k in enumerate(FAR):
            take_z(src, k)
            if place >= 1:
                relay_x(src, FAR[place - 1])
        relay_x(src, FAR[-1])
        up[z, x] = src[...]

    scaling = HD ** -0.5
    end0 = seg_ref[0, 0]
    end1 = end0 + seg_ref[0, 1]
    end2 = end1 + seg_ref[0, 2]

    def seg_of(axis):
        place = lax.broadcasted_iota(jnp.int32, (TOK, TOK), axis)
        return (jnp.where(place >= end0, 1, 0) + jnp.where(place >= end1, 1, 0)
                + jnp.where(place >= end2, 1, 0))

    def softmax():
        scores = jnp.where(seg_of(0) == seg_of(1), dot_nt(q_ref[0], k_ref[0]) * scaling, negative_big)
        shifted = jnp.exp(scores - jnp.max(scores, axis=1, keepdims=True))
        probs = shifted / jnp.sum(shifted, axis=1, keepdims=True)
        prob[...] = probs
        low[...] = probs.T.astype(BF16)
        att[...] = dot_nn(probs.astype(BF16), v_ref[0]).T.astype(BF16)

    def at_section(which, step, *args):
        @pl.when(s == which)
        def _():
            step(*args)

    wo[y] = wo_ref[0]
    wq[y] = wq_ref[0]

    @pl.when(s == 1)
    def _():
        early(up_in)

    @pl.when(s == 0)
    def _():
        late(hop)

    grad_t = jnp.zeros((HD, TOK), F32)
    for place, k in enumerate((0,) + FAR):
        finish_x(k)
        zk = (z + NZ - k) % NZ
        grad_t = grad_t + dot_nn(wo[zk], up[zk].reshape(WIDE, TOK))
        if place in (2, 4, 6):
            at_section(1, ring_step, place // 2, 2)
    grad_attn = grad_t.T.astype(BF16)
    q, k, v = q_ref[0], k_ref[0], v_ref[0]
    probs = prob[...]
    comb[:, 2 * HD:] = dot_nn(low[...], grad_attn).astype(BF16)
    grad_probs = dot_nt(grad_attn, v)
    centred = jnp.sum(probs * grad_probs, axis=1, keepdims=True)
    grad_scores = probs * (grad_probs - centred) * scaling
    comb[:, :HD] = dot_nn(grad_scores.astype(BF16), k).astype(BF16)
    comb[:, HD:2 * HD] = dot_nn(grad_scores.T.astype(BF16), q).astype(BF16)

    def grad_part(block, way):
        return dot_nt(att[...], up[block, pl.ds(2 * way, 2)].reshape(WIDE // 2, TOK))

    def grad_copy(step, way):
        toward = (y + 1) % NY if way == 0 else (y + NY - 1) % NY
        return copy(gs.at[way, step], gr.at[way, step], g_s.at[way, step], g_r.at[way, step], ring(toward))

    def grad_step(step):
        for way in (0, 1):
            if step == NY - 1:
                block = y
            else:
                block = (y + NY - 1 - step) % NY if way == 0 else (y + 1 + step) % NY
            part = grad_part(block, way)
            if step:
                arrived(gr.at[way, step - 1], g_r.at[way, step - 1])
                part = part + gr[way, step - 1].astype(F32)
            if step == NY - 1:
                ow_ref[:, pl.ds(way * WIDE // 2, WIDE // 2)] = part.astype(BF16)
            else:
                gs[way, step] = part.astype(BF16)
                grad_copy(step, way).start()

    base = s * y + (1 - s) * z

    def x_copies(m):
        j = (base + m) % NZ
        near, far = pair(m)
        return (copy(ht.at[j, across], rs1.at[m, 1], rs1_s.at[1, m], rs1_r.at[1, m], row(near)),
                copy(ht.at[j, near], rs1.at[m, 0], rs1_s.at[0, m], rs1_r.at[0, m], row(near)),
                copy(snd2.at[m], rs2.at[m], rs2_s.at[m], rs2_r.at[m], row(far)))

    def z_copy(m):
        return copy(zs.at[m], rz.at[z], rz_s.at[m], rz_r.at[z], column((base + m) % NZ))

    def term(m):
        j = (base + m) % NZ

        def one(i, _):
            ht[j, i] = dot_nt(wq[j, pl.ds(pl.multiple_of(i * COLS, COLS), COLS)], comb[...]).astype(BF16)
            return 0

        lax.fori_loop(0, NX, one, 0)
        for each in x_copies(m)[:2]:
            each.start()

    def second(m):
        j = (base + m) % NZ
        arrived(rs1.at[m, 1], rs1_r.at[1, m])
        snd2[m] = (ht[j, pair(m)[1]].astype(F32) + rs1[m, 1].astype(F32)).astype(BF16)
        x_copies(m)[2].start()

    def third(m):
        j = (base + m) % NZ
        arrived(rs1.at[m, 0], rs1_r.at[0, m])
        arrived(rs2.at[m], rs2_r.at[m])
        total = ht[j, x].astype(F32) + rs1[m, 0].astype(F32) + rs2[m].astype(F32)
        zs[m] = total.astype(BF16)

        @pl.when(j != z)
        def _():
            z_copy(m).start()

        @pl.when(j == z)
        def _():
            fin[...] = total

    def open_gate():
        pl.semaphore_signal(gate, inc=1, device_id={"section": 0}, device_id_type=MESH)

    def scatter(order, first):
        lag2, lag3 = LAGS
        for place in range(NZ + lag3):
            if first and place in (0, 1, 2):
                ring_step(1 + place, 3)
                if place == 2:
                    open_gate()
            if first and place == 5:
                parts_step(4)
            if place < NZ:
                term(order[place])
            if 0 <= place - lag2 < NZ:
                second(order[place - lag2])
            if place >= lag3:
                third(order[place - lag3])
            if not first and place % 2 == 0:
                grad_step(place // 2)

    at_section(1, scatter, (0,) + RING, True)
    at_section(0, scatter, FAR + (0,), False)
    total = fin[...] + up[z, x].astype(F32)
    for k in RING:
        src = (z + k) % NZ
        arrived(rz.at[src], rz_r.at[src])
        total = total + rz[src].astype(F32)
    og_ref[...] = total.astype(BF16)

    @pl.when(s == 1)
    def _():
        copy(og_ref, hop, hop_s.at[0], hop_r.at[0], {"section": 0}).start()
        for step in range(NY - 1):
            grad_step(step)

    grad_step(NY - 1)

    for k in RING:
        ag_z(up_in, k).wait_send()
    for k in range(NZ):
        for each in ag_x(up_in, k) + x_copies(k):
            each.wait_send()

        @pl.when((base + k) % NZ != z)
        def _():
            z_copy(k).wait_send()
    for step in range(4):
        for way in (0, 1):
            for stream in streams:
                ring_hop(stream, step, way).wait_send()
    for step in range(NY - 1):
        for way in (0, 1):
            grad_copy(step, way).wait_send()

    @pl.when(s == 1)
    def _():
        copy(og_ref, hop, hop_s.at[0], hop_r.at[0], {"section": 0}).wait_send()


def per_device(grad_out, queries, key_rows, value_rows, w_qkv, w_out, seg_lengths):
    vmem = pl.BlockSpec(memory_space=pltpu.VMEM)
    dma = pltpu.SemaphoreType.DMA
    piece = (COLS, TOK)
    grad, weight = pl.pallas_call(
        kernel,
        out_shape=(jax.ShapeDtypeStruct(piece, BF16), jax.ShapeDtypeStruct((HD, WIDE), BF16)),
        in_specs=[pl.BlockSpec(memory_space=pltpu.SMEM)] + [vmem] * 6,
        out_specs=(vmem, vmem),
        scratch_shapes=[
            pltpu.VMEM((NZ, NX) + piece, BF16),
            pltpu.VMEM((NY, HD, WIDE), BF16),
            pltpu.VMEM((NY, WIDE, 3 * HD), BF16),
            pltpu.VMEM((NZ, NX) + piece, BF16),
            pltpu.VMEM((NZ, 2) + piece, BF16),
            pltpu.VMEM((NZ,) + piece, BF16),
            pltpu.VMEM((NZ,) + piece, BF16),
            pltpu.VMEM((NZ,) + piece, BF16),
            pltpu.VMEM((NZ,) + piece, BF16),
            pltpu.VMEM((2, NY - 1, HD, WIDE // 2), BF16),
            pltpu.VMEM((2, NY - 1, HD, WIDE // 2), BF16),
            pltpu.VMEM((TOK, 3 * HD), BF16),
            pltpu.VMEM((HD, TOK), BF16),
            pltpu.VMEM((TOK, TOK), BF16),
            pltpu.VMEM((TOK, TOK), F32),
            pltpu.VMEM(piece, BF16),
            pltpu.VMEM(piece, F32),
            dma((NZ,)), dma((NZ,)), dma((3, NZ)), dma((3, NZ)),
            dma((2, 4)), dma((2, 4)), dma((3, 2, 4)), dma((3, 2, 4)),
            dma((2, NZ)), dma((2, NZ)), dma((NZ,)), dma((NZ,)),
            dma((NZ,)), dma((NZ,)), dma((2, NY - 1)), dma((2, NY - 1)), dma((1,)), dma((1,)),
            pltpu.SemaphoreType.REGULAR,
        ],
        compiler_params=pltpu.CompilerParams(collective_id=0, has_side_effects=True),
    )(seg_lengths, grad_out.T, queries, key_rows, value_rows, w_qkv, w_out)
    return grad.T[None], weight[None]


def solution(mesh):
    return jax.shard_map(
        per_device,
        mesh=mesh,
        in_specs=(
            P("dp", "tensor"),
            P("section", "dp", "tensor"),
            P("section", "dp", "tensor"),
            P("section", "dp", "tensor"),
            P("section", "dp", "tensor"),
            P("section", "tensor", "dp"),
            P("dp", None),
        ),
        out_specs=(P("section", "dp", "tensor"), P("section", "tensor", "dp")),
        check_vma=False,
    )
```

time: 190 us -> 149 us (0.78)
  the two profiles are of different devices: /device:TPU:32 before, /device:TPU:6 now
where the time goes in v2:
time: 149 us
  Pallas kernels  146 us (98%)
  local copies, waits for them, and re-layouts  2.26 us (2%)
    pallas_call x1, Pallas kernels, per_device(): pl.pallas_call(kernel, out_shape=(jax.ShapeDtypeStruct(piece, BF16), jax....  146 us

profile of v2, /device:TPU:6, one launch (start us, length us, event | category | flops | bytes accessed | tf_op | source)
XLA Modules:
  0.0 148.6 jit_solution(10800384709309809075)
XLA Ops:
  0.6 145.7 %shard_map.86 = (bf16[192,256]{1,0:T(8,128)(2,1)}, bf16[128,768]{1,0:T(8,128)(2,1)}) custom-call(s32[1,3]{1,0:T(1,128)} %seg_ref.1, bf16[192,256]{1,0:T(8,128)(2,1)} %bitcast.7, bf16[1,256,128]{2,1,0:T(8,128)(2,1)} %q_ref.1, bf16[1,256,128]{2,1,0:T(8,128)(2,1)} %k_ref.1, bf16[1,256,128]{2,1,0:T(8,128)(2,1)} %v_ref.1, bf16[1,768,384]{2,1,0:T(8,128)(2,1)} %wq_ref.1, ...), custom_call_target="tpu_custom_call" | custom-call | tf_op jit(solution)/shard_map/pallas_call | solution.py:350
  146.4 0.0 copy-start
  146.4 1.6 %copy.11 = bf16[1,256,192]{1,2,0:T(8,128)(2,1)} copy(bf16[1,256,192]{1,2,0:T(8,128)(2,1)} %bitcast.6) | data formatting | bytes 196608
  148.0 0.0 copy-done
  148.0 0.7 copy.12
Async XLA Ops:
  146.4 1.6 %copy-start = (bf16[128,768]{1,0:T(8,128)(2,1)S(1)}, bf16[128,768]{1,0:T(8,128)(2,1)}, u32[]{:S(2)}) copy-start(bf16[128,768]{1,0:T(8,128)(2,1)} %get-tuple-element.5) | copy-start | bytes 589828

commit v3 on v2

--- a/solution.py
+++ b/solution.py
@@ -11,7 +11,9 @@
 WIDE = NX * COLS
 RING = (1, 7, 2, 6, 3, 5, 4)
 FAR = (4, 3, 5, 2, 6, 1, 7)
-LAGS = (3, 6)
+TAKE = (5, 7, 1, 6, 2, 3, 4)
+LAGS = (4, 7)
+GRAD_AT = {0: 0, 4: 1, 6: 2, 8: 3, 10: 4, 12: 5, 14: 6}
 CHUNK = 256
 negative_big = -1e30
 F32, BF16 = jnp.float32, jnp.bfloat16
@@ -26,9 +28,9 @@
 
 
 def kernel(seg_ref, up_in, q_ref, k_ref, v_ref, wq_ref, wo_ref, og_ref, ow_ref,
-           up, wo, wq, ht, rs1, snd2, rs2, zs, rz, gs, gr, comb, att, low, prob, hop, fin,
+           up, wo, wq, ht, rs1, snd2, rs2, zs, rz, gs, gr, comb, att, low, prob, fin,
            agz_s, agz_r, agx_s, agx_r, wo_s, wo_r, wq_s, wq_r, rs1_s, rs1_r, rs2_s, rs2_r,
-           rz_s, rz_r, g_s, g_r, hop_s, hop_r, gate):
+           rz_s, rz_r, g_s, g_r, hop_s, gate):
     s = lax.axis_index("section")
     t = lax.axis_index("tensor")
     y = lax.axis_index("dp")
@@ -57,7 +59,8 @@
     barrier = pltpu.get_barrier_semaphore()
     peers = [row(flip), row(mirror), {"section": 1 - s}]
     peers += [column((z + k) % NZ) for k in range(1, NZ)]
-    peers += [ring((y + k) % NY) for k in range(1, NY)]
+    peers += [{"section": 1 - s, **column((z + k) % NZ)} for k in TAKE[:-1]]
+    peers += [ring((y + k) % NY) for k in (1, NY - 1)]
     for peer in peers:
         pl.semaphore_signal(barrier, inc=1, device_id=peer, device_id_type=MESH)
     pl.semaphore_wait(barrier, len(peers))
@@ -65,17 +68,27 @@
     def ag_z(src, k):
         return copy(src, up.at[z, x], agz_s.at[k], agz_r.at[k], column((z + k) % NZ))
 
+    def ag_relay(k):
+        zk = (z + 3) % NZ
+        return copy(up.at[zk, x], up.at[zk, x], agz_s.at[k], agz_r.at[k], column((z + NZ - 1) % NZ))
+
+    def pass_on(k):
+        where = {"section": 0, **column((z + k) % NZ)}
+        return copy(og_ref, up.at[z, x], hop_s.at[k], agz_r.at[k], where)
+
     def ag_x(src, k):
         zk = (z + NZ - k) % NZ
-        own = src if k == 0 else up.at[zk, x]
+        own = src if k == 0 and src is not None else up.at[zk, x]
         near, far = pair(k)
         return (copy(own, up.at[zk, x], agx_s.at[0, k], agx_r.at[0, k], row(near)),
                 copy(own, up.at[zk, x], agx_s.at[1, k], agx_r.at[1, k], row(far)),
                 copy(up.at[zk, near], up.at[zk, near], agx_s.at[2, k], agx_r.at[2, k], row(far)))
 
     def take_z(src, k):
-        if k:
+        if k or src is None:
             arrived(up.at[(z + NZ - k) % NZ, x], agz_r.at[k])
+        if k == 5:
+            ag_relay(4).start()
         for each in ag_x(src, k)[:2]:
             each.start()
 
@@ -120,20 +133,29 @@
         for index in (1, 2, 3):
             ring_step(index, step)
 
+    def gather(src, between):
+        take_z(src, 0)
+        if src is not None:
+            softmax()
+        between(-1)
+        relay_x(src, 0)
+        for place, k in enumerate(TAKE):
+            take_z(src, k)
+            if place >= 1:
+                relay_x(src, TAKE[place - 1])
+            between(place)
+        relay_x(src, TAKE[-1])
+
     def early(src):
-        for k in FAR:
+        for k in TAKE[:-1]:
             ag_z(src, k).start()
         ring_step(0, 0)
         ring_step(1, 0)
-        take_z(src, 0)
-        softmax()
-        ring_step(0, 1)
-        ring_step(2, 0)
-        relay_x(src, 0)
-        for place, k in enumerate(FAR):
-            take_z(src, k)
-            if place >= 1:
-                relay_x(src, FAR[place - 1])
+
+        def between(place):
+            if place == -1:
+                ring_step(0, 1)
+                ring_step(2, 0)
             if place == 1:
                 ring_step(0, 2)
                 ring_step(3, 0)
@@ -142,28 +164,29 @@
                 ring_step(1, 1)
             if place == 5:
                 ring_step(2, 1)
-        relay_x(src, FAR[-1])
+
+        gather(src, between)
         ring_step(3, 1)
         ring_step(0, 4)
         up[z, x] = src[...]
 
-    def late(src):
+    def late():
         softmax()
         pl.semaphore_wait(gate, 1)
-        for step in range(5):
+        for step in range(3):
             ring_step(0, step)
             parts_step(step)
-        arrived(hop, hop_r.at[0])
-        for k in FAR:
-            ag_z(src, k).start()
-        take_z(src, 0)
-        relay_x(src, 0)
-        for place, k in enumerate(FAR):
-            take_z(src, k)
-            if place >= 1:
-                relay_x(src, FAR[place - 1])
-        relay_x(src, FAR[-1])
-        up[z, x] = src[...]
+        ring_step(0, 3)
+
+        def between(place):
+            if place in (1, 3, 5):
+                ring_step(1 + place // 2, 3)
+
+        gather(None, between)
+        ring_step(0, 4)
+
+    def open_gate():
+        pl.semaphore_signal(gate, inc=1, device_id={"section": 0}, device_id_type=MESH)
 
     scaling = HD ** -0.5
     end0 = seg_ref[0, 0]
@@ -197,10 +220,10 @@
 
     @pl.when(s == 0)
     def _():
-        late(hop)
+        late()
 
     grad_t = jnp.zeros((HD, TOK), F32)
-    for place, k in enumerate((0,) + FAR):
+    for place, k in enumerate((0,) + TAKE):
         finish_x(k)
         zk = (z + NZ - k) % NZ
         grad_t = grad_t + dot_nn(wo[zk], up[zk].reshape(WIDE, TOK))
@@ -283,26 +306,23 @@
         def _():
             fin[...] = total
 
-    def open_gate():
-        pl.semaphore_signal(gate, inc=1, device_id={"section": 0}, device_id_type=MESH)
-
     def scatter(order, first):
         lag2, lag3 = LAGS
         for place in range(NZ + lag3):
             if first and place in (0, 1, 2):
                 ring_step(1 + place, 3)
-                if place == 2:
+            if place == (5 if first else 0):
+                parts_step(4)
+                if first:
                     open_gate()
-            if first and place == 5:
-                parts_step(4)
             if place < NZ:
                 term(order[place])
             if 0 <= place - lag2 < NZ:
                 second(order[place - lag2])
             if place >= lag3:
                 third(order[place - lag3])
-            if not first and place % 2 == 0:
-                grad_step(place // 2)
+            if not first and place in GRAD_AT:
+                grad_step(GRAD_AT[place])
 
     at_section(1, scatter, (0,) + RING, True)
     at_section(0, scatter, FAR + (0,), False)
@@ -315,14 +335,14 @@
 
     @pl.when(s == 1)
     def _():
-        copy(og_ref, hop, hop_s.at[0], hop_r.at[0], {"section": 0}).start()
+        for k in (0,) + TAKE[:-1]:
+            pass_on(k).start()
         for step in range(NY - 1):
             grad_step(step)
 
     grad_step(NY - 1)
 
-    for k in RING:
-        ag_z(up_in, k).wait_send()
+    ag_relay(4).wait_send()
     for k in range(NZ):
         for each in ag_x(up_in, k) + x_copies(k):
             each.wait_send()
@@ -340,7 +360,10 @@
 
     @pl.when(s == 1)
     def _():
-        copy(og_ref, hop, hop_s.at[0], hop_r.at[0], {"section": 0}).wait_send()
+        for k in TAKE[:-1]:
+            ag_z(up_in, k).wait_send()
+        for k in (0,) + TAKE[:-1]:
+            pass_on(k).wait_send()
 
 
 def per_device(grad_out, queries, key_rows, value_rows, w_qkv, w_out, seg_lengths):
@@ -368,12 +391,11 @@
             pltpu.VMEM((HD, TOK), BF16),
             pltpu.VMEM((TOK, TOK), BF16),
             pltpu.VMEM((TOK, TOK), F32),
-            pltpu.VMEM(piece, BF16),
             pltpu.VMEM(piece, F32),
             dma((NZ,)), dma((NZ,)), dma((3, NZ)), dma((3, NZ)),
             dma((2, 4)), dma((2, 4)), dma((3, 2, 4)), dma((3, 2, 4)),
             dma((2, NZ)), dma((2, NZ)), dma((NZ,)), dma((NZ,)),
-            dma((NZ,)), dma((NZ,)), dma((2, NY - 1)), dma((2, NY - 1)), dma((1,)), dma((1,)),
+            dma((NZ,)), dma((NZ,)), dma((2, NY - 1)), dma((2, NY - 1)), dma((NZ,)),
             pltpu.SemaphoreType.REGULAR,
         ],
         compiler_params=pltpu.CompilerParams(collective_id=0, has_side_effects=True),

time: 149 us -> 135 us (0.906)
  Pallas kernels: 146 us -> 131 us
    pallas_call x1, Pallas kernels: 146 us -> 131 us  [per_device(): pl.pallas_call(kernel, out_shape=(jax.ShapeDtypeStruct(piece, BF16), jax....]
where the time goes in v3:
time: 135 us; the launch traced here: 134 us
  Pallas kernels  131 us (97%)
  local copies, waits for them, and re-layouts  2.26 us (2%)
    pallas_call x1, Pallas kernels, per_device(): pl.pallas_call(kernel, out_shape=(jax.ShapeDtypeStruct(piece, BF16), jax....  131 us

profile of v3, /device:TPU:6, one launch (start us, length us, event | category | flops | bytes accessed | tf_op | source)
XLA Modules:
  0.0 134.3 jit_solution(11992047927495229081)
XLA Ops:
  0.6 131.3 %shard_map.86 = (bf16[192,256]{1,0:T(8,128)(2,1)}, bf16[128,768]{1,0:T(8,128)(2,1)}) custom-call(s32[1,3]{1,0:T(1,128)} %seg_ref.1, bf16[192,256]{1,0:T(8,128)(2,1)} %bitcast.7, bf16[1,256,128]{2,1,0:T(8,128)(2,1)} %q_ref.1, bf16[1,256,128]{2,1,0:T(8,128)(2,1)} %k_ref.1, bf16[1,256,128]{2,1,0:T(8,128)(2,1)} %v_ref.1, bf16[1,768,384]{2,1,0:T(8,128)(2,1)} %wq_ref.1, ...), custom_call_target="tpu_custom_call" | custom-call | tf_op jit(solution)/shard_map/pallas_call | solution.py:373
  132.0 0.0 copy-start
  132.0 1.6 %copy.11 = bf16[1,256,192]{1,2,0:T(8,128)(2,1)} copy(bf16[1,256,192]{1,2,0:T(8,128)(2,1)} %bitcast.6) | data formatting | bytes 196608
  133.6 0.0 copy-done
  133.6 0.7 copy.12
Async XLA Ops:
  132.0 1.6 %copy-start = (bf16[128,768]{1,0:T(8,128)(2,1)S(1)}, bf16[128,768]{1,0:T(8,128)(2,1)}, u32[]{:S(2)}) copy-start(bf16[128,768]{1,0:T(8,128)(2,1)} %get-tuple-element.5) | copy-start | bytes 589828
